TPU v7x, 512 devices: a whole 4x8x8 slice. The times are simulated.
512 devices in a mesh: row: 16 (over y, core), col: 32 (over z, x).
Axes of the slice: x: 4, y: 8, z: 8, core: 2. Of those that a mesh axis runs over, the one named last changes fastest.
Arguments:
- row_points: bfloat16 [64, 4096], P(None, 'row'), may hold values from -6 to 6
- col_points: bfloat16 [64, 262144], P(None, 'col'), may hold values from -6 to 6
- random_panel: bfloat16 [262144, 128], P('col'), may hold values from -6 to 6
Outputs:
- left_basis: float32 [4096, 128], P('row')
- coefficients: bfloat16 [128, 262144], P('row', 'col')
All inputs are finite; a program needn't handle non-finite values.
Results may differ from a plain program's by a relative error of at most 0.015.
Values may be sent and summed in bfloat16 or wider, within the bound.
A program may use at most 64 MiB of HBM per device.

v0:
```python
import math
import jax
import jax.numpy as jnp
from jax import lax
from jax.sharding import PartitionSpec as P


def kernel_tile(points_left, left_sq, col_block, exp_scale):
    cross = jnp.einsum("kr,kc->rc", points_left, col_block, preferred_element_type=jnp.float32)
    col_sq = jnp.sum(jnp.square(col_block.astype(jnp.float32)), axis=0)
    return jnp.exp((2.0 * cross - left_sq[:, None] - col_sq[None, :]) * exp_scale)


def per_device(row_points, col_points, random_panel):
    feature_dim, row_dev = row_points.shape
    col_dev, sketch_width = random_panel.shape
    exp_scale = 2.0 / feature_dim
    row_sq = jnp.sum(jnp.square(row_points.astype(jnp.float32)), axis=0)
    block_width = math.gcd(col_dev, 2048)
    block_count = col_dev // block_width
    blocks = col_points.reshape(feature_dim, block_count, block_width).transpose(1, 0, 2)
    panel_blocks = random_panel.reshape(block_count, block_width, sketch_width)
    start_sum = jnp.zeros((row_dev, sketch_width), jnp.float32)

    def add_keep(accum_sum, block_pair):
        kernel = kernel_tile(row_points, row_sq, block_pair[0], exp_scale).astype(jnp.bfloat16)
        return (
            accum_sum + jnp.dot(kernel, block_pair[1], preferred_element_type=jnp.float32),
            kernel,
        )

    partial_value, kernels = lax.scan(add_keep, start_sum, (blocks, panel_blocks))
    sketch = lax.psum(partial_value, "col")
    local_gram = jnp.dot(
        sketch.T, sketch, precision=lax.Precision.HIGHEST, preferred_element_type=jnp.float32
    )
    gram_matrix = lax.psum(local_gram, "row")
    factor = jnp.linalg.cholesky(gram_matrix)
    orthonormal = jax.scipy.linalg.solve_triangular(factor, sketch.T, lower=True).T
    left_basis = orthonormal * math.sqrt(row_dev * lax.axis_size("row"))
    orth_bf = orthonormal.astype(jnp.bfloat16)
    all_terms = jnp.einsum("rq,nrc->qnc", orth_bf, kernels, preferred_element_type=jnp.float32)
    all_terms = all_terms.reshape(sketch_width, col_dev)
    coefficients = lax.psum_scatter(
        all_terms.astype(jnp.bfloat16), "row", scatter_dimension=0, tiled=True
    )
    return (left_basis, coefficients)


def solution(mesh):
    placed = (P(None, "row"), P(None, "col"), P("col", None))
    return jax.shard_map(
        per_device,
        mesh=mesh,
        in_specs=placed,
        out_specs=(P("row", None), P("row", "col")),
        check_vma=False,
    )
```

profile of v0, /device:TPU:25, one launch (start us, length us, event | category | flops | bytes accessed | tf_op | source)
XLA Modules:
  0.0 394.3 jit_solution(6189894932676397929)
XLA Ops:
  7.2 1.9 reshape.24
  9.1 0.6 copy.16
  9.7 13.3 %while.13 = (s32[]{:T(128)}, f32[256,128]{1,0:T(8,128)S(1)}, bf16[4,256,2048]{1,2,0:T(8,128)(2,1)}, bf16[4,64,2048]{2,1,0:T(8,128)(2,1)S(1)}, bf16[64,256]{1,0:T...) while((s32[]{:T(128)}, f32[256,128]{1,0:T(8,128)S(1)}, ...), condition=%wide.region_3.4_spmd.clone, body=%wide.region_1.3_spmd.clone.sunk | while | flops 204404736 | bytes 4508267 | solution.py:32
  9.7 0.1 multiply_reduce_fusion.3
  9.8 1.7 bitcast_dynamic-update-slice_fusion.2
  11.5 1.5 convolution_add_fusion.2
  13.1 0.1 multiply_reduce_fusion.3
  13.1 1.7 bitcast_dynamic-update-slice_fusion.2
  14.9 1.5 convolution_add_fusion.2
  16.4 0.1 multiply_reduce_fusion.3
  16.5 1.7 bitcast_dynamic-update-slice_fusion.2
  18.2 1.5 convolution_add_fusion.2
  19.7 0.1 multiply_reduce_fusion.3
  19.8 1.7 bitcast_dynamic-update-slice_fusion.2
  21.5 1.5 convolution_add_fusion.2
  23.1 0.6 copy-done
  23.7 0.0 all-reduce.5.cloned.1.call-start
  23.8 154.0 %all-reduce.3.cloned.1.call-done = f32[256,128]{1,0:T(8,128)} async-done(((f32[256,128]{1,0:T(8,128)}), f32[256,128]{1,0:T(8,128)}) %all-reduce.3.cloned.1.call-update) | async-done | bytes 131088 | tf_op jit(solution)/shard_map/psum | solution.py:33
  177.8 2.0 fusion.17
  179.8 0.0 reduce-scatter.4.cloned.1.call-start
  179.9 109.6 %all-reduce.5.cloned.1.call-done = f32[128,128]{0,1:T(8,128)} async-done(((f32[128,128]{0,1:T(8,128)}), f32[128,128]{0,1:T(8,128)}) %all-reduce.5.cloned.1.call-update) | async-done | bytes 65552 | tf_op jit(solution)/shard_map/psum | solution.py:37
  289.5 0.9 copy.18
  290.5 0.9 fusion.15
  291.3 11.7 %cholesky.16 = f32[128,128]{1,0:T(8,128)S(1)} custom-call(f32[128,128]{1,0:T(8,128)S(1)} %fusion.15), custom_call_target="Cholesky" | custom-call | tf_op jit(solution)/shard_map/jit(cholesky)/cholesky | solution.py:38
  303.1 0.6 compare_reduce_fusion
  303.7 0.7 fusion.11
  304.4 9.8 %custom-call.7 = f32[1,128,128]{1,2,0:T(8,128)S(1)} custom-call(f32[1,128,128]{2,1,0:T(8,128)S(1)} %fusion.11), custom_call_target="InvertDiagBlocksLowerTriangular" | custom-call | tf_op jit(solution)/shard_map/jit(_solve_triangular)/triangular_solve | solution.py:39
  314.2 1.8 broadcast_multiply_fusion
  316.0 3.7 convolution_convert_fusion
  319.7 2.5 copy.21
  322.2 4.1 %copy.27 = bf16[128,8192]{1,0:T(8,128)(2,1)} copy(bf16[128,8192]{0,1:T(8,128)(2,1)} %bitcast.49) | data formatting | bytes 4194304
  326.3 61.5 %reduce-scatter.4.cloned.1.call-done = bf16[8,8192]{1,0:T(8,128)(2,1)} async-done(((bf16[128,8192]{1,0:T(8,128)(2,1)}), bf16[8,8192]{1,0:T(8,128)(2,1)}) %reduce-scatter.4.cloned.1.call-update) | async-done | bytes 131088
  (11 shorter events, 0.2 us)
Async XLA Ops:
  7.2 170.7 %all-reduce.3.cloned.1.call-start = ((), (), s32[]{:S(2)}) async-start(), calls=%async_computation.1 | async-start | bytes 262144 | tf_op jit(solution)/shard_map/psum | solution.py:33
  7.2 2.5 copy-start.1
  23.1 0.7 copy-start
  23.7 265.8 %all-reduce.5.cloned.1.call-start = ((), (), s32[]{:S(2)}) async-start(), calls=%async_computation.2 | async-start | bytes 131072 | tf_op jit(solution)/shard_map/psum | solution.py:37
  179.8 208.0 %reduce-scatter.4.cloned.1.call-start = ((), (), s32[]{:S(2)}) async-start(), calls=%async_computation.3 | async-start | bytes 2228224
Sparse Core Ops, SparseCore 0:
  23.9 153.9 all-reduce.2
  180.7 108.7 all-reduce.4
  326.5 61.2 reduce-scatter.3
where the time goes:
time: 395 us; the launch traced here: 394 us
  waiting for transfers between devices  325 us (82%)
  other arithmetic  24 us (6%)
  matrix products  20.4 us (5%)
  between operations  13.8 us (3%)
  local copies, waits for them, and re-layouts  10.6 us (3%)
    psum x1, waiting for transfers between devices, per_device(): sketch = lax.psum(partial_value, 'col')  154 us
    psum x1, waiting for transfers between devices, per_device(): gram_matrix = lax.psum(local_gram, 'row')  110 us
    unnamed x4, waiting for transfers between devices  61.5 us
    another operation x3, other arithmetic, per_device(): factor = jnp.linalg.cholesky(gram_matrix)  12.4 us
    another operation x2, other arithmetic, per_device(): jax.scipy.linalg.solve_triangular(factor, sketch.T, lower=True)  10.5 us
  transfers between devices with their start and end apart: 3, of which 3 were waited for; matrix products, arithmetic and copies ran while one was open for 0% of the time, Pallas kernels for 0%

commit v1 on v0

--- a/solution.py
+++ b/solution.py
@@ -30,7 +30,8 @@
         )
 
     partial_value, kernels = lax.scan(add_keep, start_sum, (blocks, panel_blocks))
-    sketch = lax.psum(partial_value, "col")
+    shards = lax.all_gather(partial_value, "col", axis=0, tiled=False)
+    sketch = shards.sum(axis=0)
     local_gram = jnp.dot(
         sketch.T, sketch, precision=lax.Precision.HIGHEST, preferred_element_type=jnp.float32
     )

time: 395 us -> 327 us (0.83)
  waiting for transfers between devices: 325 us -> 257 us
    psum x1 -> x0, waiting for transfers between devices: 154 us -> none  [per_device(): sketch = lax.psum(partial_value, 'col')]
    all_gather x0 -> x1, waiting for transfers between devices: none -> 88.8 us  [per_device(): shards = lax.all_gather(partial_value, 'col', axis=0, tiled=False)]
where the time goes in v1:
time: 327 us; the launch traced here: 326 us
  waiting for transfers between devices  257 us (79%)
  other arithmetic  26.4 us (8%)
  matrix products  18.5 us (6%)
  between operations  13.8 us (4%)
  local copies, waits for them, and re-layouts  10.6 us (3%)
    psum x1, waiting for transfers between devices, per_device(): gram_matrix = lax.psum(local_gram, 'row')  106 us
    all_gather x1, waiting for transfers between devices, per_device(): shards = lax.all_gather(partial_value, 'col', axis=0, tiled=False)  88.8 us
    unnamed x4, waiting for transfers between devices  61.5 us
    another operation x3, other arithmetic, per_device(): factor = jnp.linalg.cholesky(gram_matrix)  12.4 us
    another operation x2, other arithmetic, per_device(): jax.scipy.linalg.solve_triangular(factor, sketch.T, lower=True)  10.5 us
    dot_general x4, matrix products, kernel_tile(): jnp.einsum('kr,kc->rc', points_left, col_block, preferred_element_type=jn...  6.73 us
  transfers between devices with their start and end apart: 3, of which 3 were waited for; matrix products, arithmetic and copies ran while one was open for 0% of the time, Pallas kernels for 0%

profile of v1, /device:TPU:25, one launch (start us, length us, event | category | flops | bytes accessed | tf_op | source)
XLA Modules:
  0.0 326.5 jit_solution(10240326586997574989)
XLA Ops:
  7.2 1.9 reshape.24
  9.1 0.6 copy.16
  9.7 13.3 %while.13 = (s32[]{:T(128)}, f32[256,128]{1,0:T(8,128)S(1)}, bf16[4,256,2048]{1,2,0:T(8,128)(2,1)}, bf16[4,64,2048]{2,1,0:T(8,128)(2,1)S(1)}, bf16[64,256]{1,0:T...) while((s32[]{:T(128)}, f32[256,128]{1,0:T(8,128)S(1)}, ...), condition=%wide.region_3.4_spmd.clone, body=%wide.region_1.3_spmd.clone.sunk | while | flops 204404736 | bytes 4508267 | solution.py:32
  9.7 0.1 multiply_reduce_fusion.3
  9.8 1.7 bitcast_dynamic-update-slice_fusion.2
  11.5 1.5 convolution_add_fusion.2
  13.1 0.1 multiply_reduce_fusion.3
  13.1 1.7 bitcast_dynamic-update-slice_fusion.2
  14.9 1.5 convolution_add_fusion.2
  16.4 0.1 multiply_reduce_fusion.3
  16.5 1.7 bitcast_dynamic-update-slice_fusion.2
  18.2 1.5 convolution_add_fusion.2
  19.7 0.1 multiply_reduce_fusion.3
  19.8 1.7 bitcast_dynamic-update-slice_fusion.2
  21.5 1.5 convolution_add_fusion.2
  23.1 0.6 copy-done
  23.8 88.8 %all-gather.3.cloned.1.call-done = f32[8192,128]{1,0:T(8,128)} async-done(((f32[256,128]{1,0:T(8,128)}), f32[8192,128]{1,0:T(8,128)}) %all-gather.3.cloned.1.call-update) | async-done | bytes 4194320 | tf_op jit(solution)/shard_map/all_gather | solution.py:33
  112.6 2.4 reduce_sum.28
  115.0 1.0 fusion.17
  116.0 0.0 reduce-scatter.4.cloned.1.call-start
  116.1 106.5 %all-reduce.2.cloned.1.call-done = f32[128,128]{0,1:T(8,128)} async-done(((f32[128,128]{0,1:T(8,128)}), f32[128,128]{0,1:T(8,128)}) %all-reduce.2.cloned.1.call-update) | async-done | bytes 65552 | tf_op jit(solution)/shard_map/psum | solution.py:38
  222.6 0.9 copy.18
  223.5 0.9 fusion.15
  224.4 11.7 %cholesky.16 = f32[128,128]{1,0:T(8,128)S(1)} custom-call(f32[128,128]{1,0:T(8,128)S(1)} %fusion.15), custom_call_target="Cholesky" | custom-call | tf_op jit(solution)/shard_map/jit(cholesky)/cholesky | solution.py:39
  236.1 0.6 compare_reduce_fusion
  236.8 0.7 fusion.11
  237.4 9.8 %custom-call.7 = f32[1,128,128]{1,2,0:T(8,128)S(1)} custom-call(f32[1,128,128]{2,1,0:T(8,128)S(1)} %fusion.11), custom_call_target="InvertDiagBlocksLowerTriangular" | custom-call | tf_op jit(solution)/shard_map/jit(_solve_triangular)/triangular_solve | solution.py:40
  247.2 0.9 broadcast_multiply_fusion
  248.2 3.7 %convolution_convert_fusion = bf16[128,4,2048]{2,0,1:T(8,128)(2,1)S(1)} fusion(bf16[4,256,2048]{1,2,0:T(8,128)(2,1)} %get-tuple-element.41, bf16[256,128]{1,0:T(8,128)(2,1)S(1)} %get-tuple-element.101), kind=kOutput, calls=%fused_computation.15 | convolution fusion | flops 537919488 | bytes 6356992 | tf_op jit(solution)/shard_map/rq,nrc->qnc/dot_general | solution.py:43
  251.8 2.5 copy.21
  254.4 4.1 %copy.27 = bf16[128,8192]{1,0:T(8,128)(2,1)} copy(bf16[128,8192]{0,1:T(8,128)(2,1)} %bitcast.50) | data formatting | bytes 4194304
  258.5 61.5 %reduce-scatter.4.cloned.1.call-done = bf16[8,8192]{1,0:T(8,128)(2,1)} async-done(((bf16[128,8192]{1,0:T(8,128)(2,1)}), bf16[8,8192]{1,0:T(8,128)(2,1)}) %reduce-scatter.4.cloned.1.call-update) | async-done | bytes 131088
  (12 shorter events, 0.2 us)
Async XLA Ops:
  7.2 105.4 %all-gather.3.cloned.1.call-start = ((), (), s32[]{:S(2)}) async-start(), calls=%async_computation.2 | async-start | bytes 4325376 | tf_op jit(solution)/shard_map/all_gather | solution.py:33
  7.2 2.5 copy-start.1
  23.1 0.7 copy-start
  23.7 198.8 %all-reduce.2.cloned.1.call-start = ((), (), s32[]{:S(2)}) async-start(), calls=%async_computation.1 | async-start | bytes 131072 | tf_op jit(solution)/shard_map/psum | solution.py:38
  116.0 203.9 %reduce-scatter.4.cloned.1.call-start = ((), (), s32[]{:S(2)}) async-start(), calls=%async_computation.3 | async-start | bytes 2228224
Sparse Core Ops, SparseCore 0:
  23.9 88.7 all-gather.2
  116.2 106.3 all-reduce.1
  258.6 61.2 reduce-scatter.3
